TPU v7x, 32 devices: a whole 2x2x4 slice. The times are simulated.
32 devices in a mesh: blk: 8 (over y, x, core), feat: 4 (over z).
Axes of the slice: x: 2, y: 2, z: 4, core: 2. Of those that a mesh axis runs over, the one named last changes fastest.
Arguments:
- node_feats: bfloat16 [8192, 512], P('blk', 'feat'), may hold values from -6 to 6
- weight: bfloat16 [512, 512], P(None, 'feat'), may hold values from -0.25 to 0.25
- tile_value: bfloat16 [8, 5, 8, 128, 128], P('blk'), may hold values from -0.75 to 0.75
- tile_row: int32 [8, 5, 8], P('blk'), may hold values from 0 to 7
- tile_col: int32 [8, 5, 8], P('blk'), may hold values from 0 to 7
- tile_count: int32 [8, 5], P('blk'), may hold values from 2 to 8, as said below
- grad_out: bfloat16 [8192, 512], P('blk', 'feat'), may hold values from -6 to 6
Outputs:
- output_y: bfloat16 [8192, 512], P('blk', 'feat')
- grad_x: bfloat16 [8192, 512], P('blk', 'feat')
- grad_w: float32 [512, 512], P(None, 'feat')
Inputs may be any that keep to these rules, and one draw needn't show every extreme that they name: `tile_count`: in every draw one owner has all 8 slots live for every distance; owners differ in how many tiles they hold.
All inputs are finite; a program needn't handle non-finite values.
Results may differ from a plain program's by a relative error of at most 0.0062.
Values may be sent and summed in bfloat16 or wider, within the bound.
A program may use at most 64 MiB of HBM per device.

v0:
```python
import jax
import jax.numpy as jnp
from jax import lax
from jax.sharding import PartitionSpec as P


def shifted(block, axis, distance):
    devices = range(lax.axis_size(axis))
    route = [((i - distance) % len(devices), i) for i in devices]
    return lax.ppermute(block, axis, route)


def on_device(node_feats, weight, tile_value, tile_row, tile_col, tile_count, grad_out):
    tile_side = tile_value.shape[-1]
    blocks = node_feats.shape[0] // tile_side
    feat_width = weight.shape[1]
    offsets = tile_value.shape[1]
    reach_count = (offsets - 1) // 2
    slot_ids = jnp.arange(tile_value.shape[2], dtype=jnp.int32)
    block_ids = jnp.arange(blocks, dtype=jnp.int32)
    live_slots = slot_ids[None, :] < tile_count[0][:, None]
    row_onehot = (
        (tile_row[0][:, None, :] == block_ids[None, :, None]) & live_slots[:, None, :]
    ).astype(jnp.float32)
    col_onehot = (
        (tile_col[0][:, None, :] == block_ids[None, :, None]) & live_slots[:, None, :]
    ).astype(jnp.float32)
    full_feats = lax.all_gather(node_feats, "feat", axis=1, tiled=True)
    hidden = jnp.dot(full_feats, weight, preferred_element_type=jnp.float32).astype(jnp.bfloat16)
    panel_own = hidden.reshape(blocks, tile_side, feat_width)
    wanted_lists = {}
    picked = jnp.take(panel_own, tile_col[0, reach_count], axis=0)
    gather_product = jnp.einsum(
        "sij,sjf->sif", tile_value[0, reach_count], picked, preferred_element_type=jnp.float32
    )
    aggregate = jnp.einsum(
        "rs,sif->rif", row_onehot[reach_count], gather_product, precision=lax.Precision.HIGHEST
    )
    for distance in range(-reach_count, reach_count + 1):
        if distance != 0:
            offset = distance + reach_count
            wanted = shifted(tile_col[0, offset], "blk", distance)
            wanted_lists[distance] = wanted
            sent_blocks = jnp.take(panel_own, wanted, axis=0)
            arrived = shifted(sent_blocks, "blk", -distance)
            product = jnp.einsum(
                "sij,sjf->sif", tile_value[0, offset], arrived, preferred_element_type=jnp.float32
            )
            aggregate = aggregate + jnp.einsum(
                "rs,sif->rif", row_onehot[offset], product, precision=lax.Precision.HIGHEST
            )
    preact = aggregate.reshape(blocks * tile_side, feat_width) + hidden.astype(jnp.float32)
    output_y = jax.nn.silu(preact).astype(jnp.bfloat16)
    sigmoid_pre = jax.nn.sigmoid(preact)
    slope_term = sigmoid_pre * (1.0 + preact * (1.0 - sigmoid_pre))
    grad_pre = (grad_out.astype(jnp.float32) * slope_term).astype(jnp.bfloat16)
    grad_blocks = grad_pre.reshape(blocks, tile_side, feat_width)

    def slot_products(offset):
        picked = jnp.take(grad_blocks, tile_row[0, offset], axis=0)
        return jnp.einsum(
            "sji,sjf->sif", tile_value[0, offset], picked, preferred_element_type=jnp.float32
        )

    transposed = jnp.einsum(
        "cs,sif->cif",
        col_onehot[reach_count],
        slot_products(reach_count),
        precision=lax.Precision.HIGHEST,
    )
    for distance in range(-reach_count, reach_count + 1):
        if distance != 0:
            offset = distance + reach_count
            masked = slot_products(offset) * live_slots[offset][:, None, None].astype(jnp.float32)
            received = shifted(masked, "blk", distance)
            target_onehot = (wanted_lists[distance][None, :] == block_ids[:, None]).astype(
                jnp.float32
            )
            transposed = transposed + jnp.einsum(
                "cs,sif->cif", target_onehot, received, precision=lax.Precision.HIGHEST
            )
    grad_hidden = (
        grad_pre.astype(jnp.float32) + transposed.reshape(blocks * tile_side, feat_width)
    ).astype(jnp.bfloat16)
    weight_term = lax.dot_general(
        full_feats, grad_hidden, (((0,), (0,)), ((), ())), preferred_element_type=jnp.float32
    )
    grad_w = lax.psum(weight_term, "blk")
    partial_grad = lax.dot_general(
        grad_hidden, weight, (((1,), (1,)), ((), ())), preferred_element_type=jnp.float32
    )
    grad_x = lax.psum_scatter(partial_grad, "feat", scatter_dimension=1, tiled=True).astype(
        jnp.bfloat16
    )
    return (output_y, grad_x, grad_w)


def solution(mesh):
    return jax.shard_map(
        on_device,
        mesh=mesh,
        in_specs=(
            P("blk", "feat"),
            P(None, "feat"),
            P("blk", None, None, None, None),
            P("blk", None, None),
            P("blk", None, None),
            P("blk", None),
            P("blk", "feat"),
        ),
        out_specs=(P("blk", "feat"), P("blk", "feat"), P(None, "feat")),
        check_vma=False,
    )
```

profile of v0, /device:TPU:0, one launch (start us, length us, event | category | flops | bytes accessed | tf_op | source)
XLA Modules:
  0.0 216.4 jit_solution(13034620834880448403)
XLA Ops:
  8.7 3.9 %collective-permute-start = (s32[8]{0:T(128)S(1)}, s32[8]{0:T(128)S(1)}, u32[]{:S(2)}, u32[]{:S(2)}) collective-permute-start(s32[8]{0:T(128)S(1)} %get-tuple-element.32), channel_id=1, source_target_pairs={{8,0},{12,4},{16,8},{20,12},{24,16},{28,20},{0,24},{4,28},{9,1},{1... | collective-permute-start | bytes 104 | tf_op jit(solution)/shard_map/ppermute | solution.py:10
  15.1 1.3 compare_and_fusion.2
  22.6 19.6 %all-gather.2.cloned.1.call-done = bf16[1024,512]{1,0:T(8,128)(2,1)} async-done(((bf16[1024,128]{1,0:T(8,128)(2,1)}), bf16[1024,512]{1,0:T(8,128)(2,1)}) %all-gather.2.cloned.1.call-update) | async-done | bytes 1048592 | tf_op jit(solution)/shard_map/all_gather | solution.py:28
  42.2 1.7 convolution_convert_fusion
  49.6 2.6 %collective-permute-start.5 = (bf16[8,128,128]{2,1,0:T(8,128)(2,1)}, bf16[8,128,128]{2,1,0:T(8,128)(2,1)}, u32[]{:S(2)}, u32[]{:S(2)}) collective-permute-start(bf16[8,128,128]{2,1,0:T(8,128)(2,1)} %broadcast_select_fusion.1), channel_id=1, source_target_pairs={{4,0},{8,4},{12,8},{16,12},{20,16},{24,20},{28,24},{0,28},{5,1},{9... | collective-permute-start | bytes 786440 | tf_op jit(solution)/shard_map/ppermute | solution.py:10
  53.7 1.3 collective-permute-start.7
  55.4 1.3 fusion.25
  56.7 1.3 fusion.21
  60.0 1.3 fusion.17
  62.3 1.8 collective-permute-done.7
  71.9 1.5 collective-permute-start.8
  81.3 2.4 %collective-permute-start.9 = (f32[8,128,128]{2,0,1:T(8,128)S(1)}, f32[8,128,128]{2,0,1:T(8,128)S(1)}, u32[]{:S(2)}, u32[]{:S(2)}) collective-permute-start(f32[8,128,128]{2,0,1:T(8,128)S(1)} %multiply_bitcast_fusion.2), channel_id=1, source_target_pairs={{4,0},{8,4},{12,8},{16,12},{20,16},{24,20},{28,24},{0,28},{5,1},{9... | collective-permute-start | bytes 1572872 | tf_op jit(solution)/shard_map/ppermute | solution.py:10
  84.1 9.4 %collective-permute-done.10 = f32[8,128,128]{2,0,1:T(8,128)} collective-permute-done((f32[8,128,128]{2,0,1:T(8,128)}, f32[8,128,128]{2,0,1:T(8,128)}, u32[]{:S(2)}, u32[]{:S(2)}) %collective-permute-start.10) | collective-permute-done | bytes 524320 | tf_op jit(solution)/shard_map/ppermute | solution.py:10
  93.4 1.4 fusion.65
  94.8 3.1 %collective-permute-done.11 = f32[8,128,128]{2,0,1:T(8,128)} collective-permute-done((f32[8,128,128]{2,0,1:T(8,128)}, f32[8,128,128]{2,0,1:T(8,128)}, u32[]{:S(2)}, u32[]{:S(2)}) %collective-permute-start.11) | collective-permute-done | bytes 524320 | tf_op jit(solution)/shard_map/ppermute | solution.py:10
  97.9 1.4 fusion.68
  99.4 1.4 convolution_add_fusion.1
  100.8 5.3 %collective-permute-done.9 = f32[8,128,128]{2,0,1:T(8,128)S(1)} collective-permute-done((f32[8,128,128]{2,0,1:T(8,128)S(1)}, f32[8,128,128]{2,0,1:T(8,128)S(1)}, u32[]{:S(2)}, u32[]{:S(2)}) %collective-permute-start.9) | collective-permute-done | bytes 524320 | tf_op jit(solution)/shard_map/ppermute | solution.py:10
  107.7 1.0 convolution_bitcast_fusion
  108.8 1.8 fusion.89
  110.6 52.1 %all-reduce.2.cloned.1.call-done = f32[512,128]{0,1:T(8,128)} async-done(((f32[512,128]{0,1:T(8,128)}), f32[512,128]{0,1:T(8,128)}) %all-reduce.2.cloned.1.call-update) | async-done | bytes 262160 | tf_op jit(solution)/shard_map/psum | solution.py:88
  162.7 1.8 copy.12
  164.5 43.6 %reduce-scatter.2.cloned.1.call-done = f32[1024,128]{1,0:T(8,128)} async-done(((f32[1024,512]{1,0:T(8,128)}), f32[1024,128]{1,0:T(8,128)}) %reduce-scatter.2.cloned.1.call-update) | async-done | bytes 524304 | tf_op jit(solution)/shard_map/reduce_scatter | solution.py:92
  208.1 1.8 convert_element_type.89
  (149 shorter events, 37.9 us)
Async XLA Ops:
  7.2 35.1 %copy-start = (bf16[512,128]{1,0:T(8,128)(2,1)S(1)}, bf16[512,128]{1,0:T(8,128)(2,1)}, u32[]{:S(2)}) copy-start(bf16[512,128]{1,0:T(8,128)(2,1)} %param.10) | copy-start | bytes 393220
  7.2 35.1 %all-gather.2.cloned.1.call-start = ((), (), s32[]{:S(2)}) async-start(), calls=%async_computation.1 | async-start | bytes 1310720 | tf_op jit(solution)/shard_map/all_gather | solution.py:28
  7.9 154.8 %all-reduce.2.cloned.1.call-start = ((), (), s32[]{:S(2)}) async-start(), calls=%async_computation.3 | async-start | bytes 524288 | tf_op jit(solution)/shard_map/psum | solution.py:88
  8.7 11.6 %collective-permute-start = (s32[8]{0:T(128)S(1)}, s32[8]{0:T(128)S(1)}, u32[]{:S(2)}, u32[]{:S(2)}) collective-permute-start(s32[8]{0:T(128)S(1)} %get-tuple-element.32), channel_id=1, source_target_pairs={{8,0},{12,4},{16,8},{20,12},{24,16},{28,20},{0,24},{4,28},{9,1},{1... | collective-permute-start | bytes 104 | tf_op jit(solution)/shard_map/ppermute | solution.py:10
  12.6 7.7 %collective-permute-start.2 = (s32[8]{0:T(128)S(1)}, s32[8]{0:T(128)S(1)}, u32[]{:S(2)}, u32[]{:S(2)}) collective-permute-start(s32[8]{0:T(128)S(1)} %get-tuple-element.31), channel_id=1, source_target_pairs={{4,0},{8,4},{12,8},{16,12},{20,16},{24,20},{28,24},{0,28},{5,1},{9... | collective-permute-start | bytes 104 | tf_op jit(solution)/shard_map/ppermute | solution.py:10
  12.6 7.7 %collective-permute-start.4 = (s32[8]{0:T(128)S(1)}, s32[8]{0:T(128)S(1)}, u32[]{:S(2)}, u32[]{:S(2)}) collective-permute-start(s32[8]{0:T(128)S(1)} %get-tuple-element.30), channel_id=1, source_target_pairs={{28,0},{0,4},{4,8},{8,12},{12,16},{16,20},{20,24},{24,28},{29,1},{... | collective-permute-start | bytes 104 | tf_op jit(solution)/shard_map/ppermute | solution.py:10
  13.1 7.8 %collective-permute-start.6 = (s32[8]{0:T(128)S(1)}, s32[8]{0:T(128)S(1)}, u32[]{:S(2)}, u32[]{:S(2)}) collective-permute-start(s32[8]{0:T(128)S(1)} %get-tuple-element.29), channel_id=1, source_target_pairs={{24,0},{28,4},{0,8},{4,12},{8,16},{12,20},{16,24},{20,28},{25,1},{... | collective-permute-start | bytes 104 | tf_op jit(solution)/shard_map/ppermute | solution.py:10
  20.2 25.7 %copy-start.19 = (s32[8]{0:T(128)}, s32[8]{0:T(128)S(1)}, u32[]{:S(2)}) copy-start(s32[8]{0:T(128)S(1)} %collective-permute-done) | copy-start | bytes 100
  20.3 25.7 %copy-start.27 = (s32[8]{0:T(128)}, s32[8]{0:T(128)S(1)}, u32[]{:S(2)}) copy-start(s32[8]{0:T(128)S(1)} %collective-permute-done.2) | copy-start | bytes 100
  20.3 25.7 %copy-start.23 = (s32[8]{0:T(128)}, s32[8]{0:T(128)S(1)}, u32[]{:S(2)}) copy-start(s32[8]{0:T(128)S(1)} %collective-permute-done.4) | copy-start | bytes 100
  20.9 25.0 %copy-start.21 = (s32[8]{0:T(128)}, s32[8]{0:T(128)S(1)}, u32[]{:S(2)}) copy-start(s32[8]{0:T(128)S(1)} %collective-permute-done.6) | copy-start | bytes 100
  22.6 23.4 %copy-start.1 = (bf16[1,5,8,128,128]{4,3,2,1,0:T(8,128)(2,1)S(1)}, bf16[1,5,8,128,128]{4,3,2,1,0:T(8,128)(2,1)}, u32[]{:S(2)}) copy-start(bf16[1,5,8,128,128]{4,3,2,1,0:T(8,128)(2,1)} %param.11) | copy-start | bytes 3932164
  44.6 10.8 %collective-permute-start.1 = (bf16[8,128,128]{2,1,0:T(8,128)(2,1)S(1)}, bf16[8,128,128]{2,1,0:T(8,128)(2,1)}, u32[]{:S(2)}, u32[]{:S(2)}) collective-permute-start(bf16[8,128,128]{2,1,0:T(8,128)(2,1)S(1)} %broadcast_select_fusion.3), channel_id=1, source_target_pairs={{24,0},{28,4},{0,8},{4,12},{8,16},{12,20},{16,24},{20,28},{25,1},{... | collective-permute-start | bytes 786440 | tf_op jit(solution)/shard_map/ppermute | solution.py:10
  48.0 8.6 %collective-permute-start.3 = (bf16[8,128,128]{2,1,0:T(8,128)(2,1)S(1)}, bf16[8,128,128]{2,1,0:T(8,128)(2,1)}, u32[]{:S(2)}, u32[]{:S(2)}) collective-permute-start(bf16[8,128,128]{2,1,0:T(8,128)(2,1)S(1)} %broadcast_select_fusion.2), channel_id=1, source_target_pairs={{28,0},{0,4},{4,8},{8,12},{12,16},{16,20},{20,24},{24,28},{29,1},{... | collective-permute-start | bytes 786440 | tf_op jit(solution)/shard_map/ppermute | solution.py:10
  49.6 10.4 %collective-permute-start.5 = (bf16[8,128,128]{2,1,0:T(8,128)(2,1)}, bf16[8,128,128]{2,1,0:T(8,128)(2,1)}, u32[]{:S(2)}, u32[]{:S(2)}) collective-permute-start(bf16[8,128,128]{2,1,0:T(8,128)(2,1)} %broadcast_select_fusion.1), channel_id=1, source_target_pairs={{4,0},{8,4},{12,8},{16,12},{20,16},{24,20},{28,24},{0,28},{5,1},{9... | collective-permute-start | bytes 786440 | tf_op jit(solution)/shard_map/ppermute | solution.py:10
  53.7 10.4 %collective-permute-start.7 = (bf16[8,128,128]{2,1,0:T(8,128)(2,1)}, bf16[8,128,128]{2,1,0:T(8,128)(2,1)S(1)}, u32[]{:S(2)}, u32[]{:S(2)}) collective-permute-start(bf16[8,128,128]{2,1,0:T(8,128)(2,1)} %broadcast_select_fusion), channel_id=1, source_target_pairs={{8,0},{12,4},{16,8},{20,12},{24,16},{28,20},{0,24},{4,28},{9,1},{1... | collective-permute-start | bytes 786440 | tf_op jit(solution)/shard_map/ppermute | solution.py:10
  71.9 27.5 %collective-permute-start.8 = (f32[8,128,128]{2,0,1:T(8,128)}, f32[8,128,128]{2,0,1:T(8,128)}, u32[]{:S(2)}, u32[]{:S(2)}) collective-permute-start(f32[8,128,128]{2,0,1:T(8,128)} %multiply_bitcast_fusion.3), channel_id=1, source_target_pairs={{8,0},{12,4},{16,8},{20,12},{24,16},{28,20},{0,24},{4,28},{9,1},{1... | collective-permute-start | bytes 1572872 | tf_op jit(solution)/shard_map/ppermute | solution.py:10
  76.2 17.2 %collective-permute-start.10 = (f32[8,128,128]{2,0,1:T(8,128)}, f32[8,128,128]{2,0,1:T(8,128)}, u32[]{:S(2)}, u32[]{:S(2)}) collective-permute-start(f32[8,128,128]{2,0,1:T(8,128)} %multiply_bitcast_fusion.1), channel_id=1, source_target_pairs={{28,0},{0,4},{4,8},{8,12},{12,16},{16,20},{20,24},{24,28},{29,1},{... | collective-permute-start | bytes 1572872 | tf_op jit(solution)/shard_map/ppermute | solution.py:10
  78.6 19.4 %collective-permute-start.11 = (f32[8,128,128]{2,0,1:T(8,128)}, f32[8,128,128]{2,0,1:T(8,128)}, u32[]{:S(2)}, u32[]{:S(2)}) collective-permute-start(f32[8,128,128]{2,0,1:T(8,128)} %multiply_bitcast_fusion), channel_id=1, source_target_pairs={{24,0},{28,4},{0,8},{4,12},{8,16},{12,20},{16,24},{20,28},{25,1},{... | collective-permute-start | bytes 1572872 | tf_op jit(solution)/shard_map/ppermute | solution.py:10
  81.0 12.4 %copy-start.24 = (s32[8]{0:T(128)S(1)}, s32[8]{0:T(128)}, u32[]{:S(2)}) copy-start(s32[8]{0:T(128)} %copy-done.23) | copy-start | bytes 100
  81.3 16.7 %copy-start.22 = (s32[8]{0:T(128)S(1)}, s32[8]{0:T(128)}, u32[]{:S(2)}) copy-start(s32[8]{0:T(128)} %copy-done.21) | copy-start | bytes 100
  81.3 24.8 %collective-permute-start.9 = (f32[8,128,128]{2,0,1:T(8,128)S(1)}, f32[8,128,128]{2,0,1:T(8,128)S(1)}, u32[]{:S(2)}, u32[]{:S(2)}) collective-permute-start(f32[8,128,128]{2,0,1:T(8,128)S(1)} %multiply_bitcast_fusion.2), channel_id=1, source_target_pairs={{4,0},{8,4},{12,8},{16,12},{20,16},{24,20},{28,24},{0,28},{5,1},{9... | collective-permute-start | bytes 1572872 | tf_op jit(solution)/shard_map/ppermute | solution.py:10
  84.1 15.3 %copy-start.20 = (s32[8]{0:T(128)S(1)}, s32[8]{0:T(128)}, u32[]{:S(2)}) copy-start(s32[8]{0:T(128)} %copy-done.19) | copy-start | bytes 100
  108.8 99.3 %reduce-scatter.2.cloned.1.call-start = ((), (), s32[]{:S(2)}) async-start(), calls=%async_computation.2 | async-start | bytes 2621440 | tf_op jit(solution)/shard_map/reduce_scatter | solution.py:92
  (20 other events, 51.7 us)
Sparse Core Ops, SparseCore 0:
  9.5 32.6 all-gather.1
  108.9 53.7 all-reduce.1
  165.0 43.0 reduce-scatter.1
where the time goes:
time: 217 us; the launch traced here: 216 us
  waiting for transfers between devices  136 us (63%)
  local copies, waits for them, and re-layouts  19.5 us (9%)
  matrix products  17.6 us (8%)
  other arithmetic  14.8 us (7%)
  starting transfers between devices  14.4 us (7%)
  between operations  14.4 us (7%)
    psum x1, waiting for transfers between devices, on_device(): grad_w = lax.psum(weight_term, 'blk')  52.1 us
    reduce_scatter x1, waiting for transfers between devices, on_device(): lax.psum_scatter(partial_grad, 'feat', scatter_dimension=1, tiled=True)  43.6 us
    all_gather x1, waiting for transfers between devices, on_device(): full_feats = lax.all_gather(node_feats, 'feat', axis=1, tiled=True)  19.6 us
    ppermute x12, waiting for transfers between devices, shifted(): return lax.ppermute(block, axis, route)  19.6 us
    ppermute x12, starting transfers between devices, shifted(): return lax.ppermute(block, axis, route)  14.3 us
    unnamed x61, local copies, waits for them, and re-layouts  5.8 us
    dot_general x4, matrix products, on_device(): jnp.einsum('cs,sif->cif', target_onehot, received, precision=lax.Precisio...  4.6 us
  transfers between devices with their start and end apart: 15, of which 7 were waited for; matrix products, arithmetic and copies ran while one was open for 17% of the time, Pallas kernels for 0%

commit v1 on v0

v1 whole, which is shorter than its diff:
```python
import functools

import jax
import jax.numpy as jnp
from jax import lax
from jax.experimental import pallas as pl
from jax.experimental.pallas import tpu as pltpu
from jax.sharding import PartitionSpec as P

MESH = pl.DeviceIdType.MESH
BF = jnp.bfloat16
F32 = jnp.float32


def stage_factors(count, rows):
    factors = []
    while count > 1:
        size = max(f for f in range(2, 17) if count % f == 0 and rows % (16 * f) == 0)
        factors.append(size)
        count //= size
    return factors


def remote(src, dst, send, recv, where):
    return pltpu.make_async_remote_copy(
        src_ref=src, dst_ref=dst, send_sem=send, recv_sem=recv, device_id=where, device_id_type=MESH
    )


def layer_kernel(
    dims, x, w, tv, tr, tc, cnt, go, y, gx, gw,
    xg, wz, tt, prod, gp, sent, got, gg, gwb, *rest
):
    nb, nz, offs, slots, blocks, side, width, ahead, factors = dims
    stages = len(factors)
    hid, rest = rest[:offs], rest[offs:]
    gathered, summed = rest[:stages], rest[stages : 2 * stages]
    (xs, xr, xl, ws, wr, hs, hr, gs, gr, zs, zr, zl) = rest[2 * stages : 2 * stages + 12]
    psems = rest[2 * stages + 12 :]
    reach = (offs - 1) // 2
    far = [k for k in range(offs) if k != reach]
    per_block = slots // blocks
    me = lax.axis_index("feat")
    own = lax.axis_index("blk")

    def rows(b):
        return pl.ds(pl.multiple_of(b * side, side), side)

    def cols(z):
        return pl.ds(pl.multiple_of(z * width, width), width)

    def blk_at(distance):
        return lax.rem(own + distance + nb, nb)

    def stage_peer(stage, step):
        stride = 1
        for f in factors[:stage]:
            stride *= f
        size = factors[stage]
        digit = lax.rem(own // stride, size)
        other = lax.rem(digit + step, size)
        return digit, other, own + (other - digit) * stride

    barrier = pltpu.get_barrier_semaphore()
    greeted = 0
    for step in range(1, nz):
        pl.semaphore_signal(barrier, inc=1, device_id={"feat": lax.rem(me + step, nz)}, device_id_type=MESH)
        greeted += 1
    for k in far if stages > 1 else ():
        pl.semaphore_signal(barrier, inc=1, device_id={"blk": blk_at(k - reach)}, device_id_type=MESH)
        greeted += 1
    for stage in range(stages):
        for step in range(1, factors[stage]):
            _, _, peer = stage_peer(stage, step)
            pl.semaphore_signal(barrier, inc=1, device_id={"blk": peer}, device_id_type=MESH)
            greeted += 1
    pl.semaphore_wait(barrier, greeted)

    def line_send(src_of, dst, send, recv, b):
        for d in (1, 2):
            for sign in (-1, 1):
                t = me + sign * d

                @pl.when((t >= 0) & (t < nz))
                def _():
                    remote(
                        src_of(b), dst.at[rows(b), cols(me)], send.at[t, b], recv.at[me, b], {"feat": t}
                    ).start()

    def line_recv(dst, relay, recv, b):
        for d in range(1, nz):
            for sign in (-1, 1):
                s = me + sign * d

                @pl.when((s >= 0) & (s < nz))
                def _():
                    piece = dst.at[rows(b), cols(s)]
                    remote(piece, piece, relay.at[s, b], recv.at[s, b], {"feat": s}).wait_recv()
                    if d >= 2:
                        t = me - sign

                        @pl.when((t >= 0) & (t < nz))
                        def _():
                            remote(piece, piece, relay.at[s, b], recv.at[s, b], {"feat": t}).start()

    def line_drain(dst, send, relay, recv, b):
        for d in (1, 2):
            for sign in (-1, 1):
                t = me + sign * d

                @pl.when((t >= 0) & (t < nz))
                def _():
                    piece = dst.at[rows(b), cols(me)]
                    remote(piece, piece, send.at[t, b], recv.at[me, b], {"feat": t}).wait_send()

        for d in range(2, nz):
            for sign in (-1, 1):
                s = me + sign * d
                t = me - sign

                @pl.when((s >= 0) & (s < nz) & (t >= 0) & (t < nz))
                def _():
                    piece = dst.at[rows(b), cols(s)]
                    remote(piece, piece, relay.at[s, b], recv.at[s, b], {"feat": t}).wait_send()

    def x_piece(b):
        return x.at[rows(b), :]

    for b in range(min(ahead, blocks)):
        line_send(x_piece, xg, xs, xr, b)
    for step in range(1, nz):
        d = lax.rem(me + step, nz)
        remote(w.at[cols(d), :], wz.at[:, cols(me)], ws.at[step], wr.at[nz - step], {"feat": d}).start()
    xg[:, cols(me)] = x[...]
    wz[:, cols(me)] = w[cols(me), :]

    def forward_step(b, carry):
        @pl.when(b + ahead < blocks)
        def _():
            line_send(x_piece, xg, xs, xr, b + ahead)

        for k in range(offs):
            for s in range(per_block):
                slot = b * per_block + s
                tt[k, slot] = tv[0, k, slot].T
        line_recv(xg, xl, xr, b)
        hid[reach][b] = jnp.dot(xg[rows(b), :], w[...], preferred_element_type=F32).astype(BF)
        for k in far:
            remote(
                hid[reach].at[b], hid[k].at[b], hs.at[k, b], hr.at[k, b], {"blk": blk_at(reach - k)}
            ).start()
        return carry

    lax.fori_loop(0, blocks, forward_step, 0)

    def forward_products(k):
        for s in range(slots):
            prod[k, s] = jnp.dot(tv[0, k, s], hid[k][tc[0, k, s]], preferred_element_type=F32)

    forward_products(reach)
    for k in far:
        for b in range(blocks):
            remote(
                hid[k].at[b], hid[k].at[b], hs.at[k, b], hr.at[k, b], {"blk": blk_at(k - reach)}
            ).wait_recv()
        forward_products(k)

    def weight_of(table, k, s, b):
        return jnp.where((table[0, k, s] == b) & (s < cnt[0, k]), 1.0, 0.0).astype(F32)

    def pointwise(b, carry):
        v = hid[reach][b].astype(F32)
        for k in range(offs):
            for s in range(slots):
                v = v + prod[k, s] * weight_of(tr, k, s, b)
        sigma = jax.nn.sigmoid(v)
        y[rows(b), :] = (v * sigma).astype(BF)
        slope = sigma * (1.0 + v * (1.0 - sigma))
        gp[b] = (go[rows(b), :].astype(F32) * slope).astype(BF)
        return carry

    lax.fori_loop(0, blocks, pointwise, 0)

    for k in range(offs):
        for s in range(slots):
            prod[k, s] = jnp.dot(tt[k, s], gp[tr[0, k, s]], preferred_element_type=F32)

    def column_sum(k, c, start):
        total = start
        for s in range(slots):
            term = prod[k, s] * weight_of(tc, k, s, c)
            total = term if total is None else total + term
        return total

    gw[...] = jnp.zeros_like(gw)

    def gg_piece(b):
        return gg.at[rows(b), cols(me)]

    def make_grad(b):
        total = column_sum(reach, b, gp[b].astype(F32))
        for k in far:
            remote(
                sent.at[k, b], got.at[k, b], gs.at[k, b], gr.at[k, b], {"blk": blk_at(reach - k)}
            ).wait_recv()
            total = total + got[k, b].astype(F32)
        grad = total.astype(BF)
        gg[rows(b), cols(me)] = grad
        line_send(gg_piece, gg, zs, zr, b)
        gw[...] += lax.dot_general(
            xg[rows(b), :], grad, (((0,), (0,)), ((), ())), preferred_element_type=F32
        )

    def finish(b):
        line_recv(gg, zl, zr, b)
        gx[rows(b), :] = lax.dot_general(
            gg[rows(b), :], wz[...], (((1,), (1,)), ((), ())), preferred_element_type=F32
        ).astype(BF)

    for step in range(1, nz):
        d = lax.rem(me + step, nz)
        piece = wz.at[:, cols(d)]
        remote(w.at[cols(d), :], piece, ws.at[step], wr.at[step], {"feat": d}).wait_recv()

    lag, tail = 1, 3

    def backward_step(c, carry):
        @pl.when(c < blocks)
        def _():
            for k in far:
                sent[k, c] = column_sum(k, c, None).astype(BF)
                remote(
                    sent.at[k, c], got.at[k, c], gs.at[k, c], gr.at[k, c], {"blk": blk_at(k - reach)}
                ).start()

        @pl.when(c >= lag)
        def _():
            make_grad(c - lag)

        @pl.when(c >= tail)
        def _():
            finish(c - tail)

        return carry

    lax.fori_loop(0, blocks + lag, backward_step, 0)

    gwb[...] = gw[...].astype(BF)
    height = gw.shape[0]
    for stage in range(stages):
        size = factors[stage]
        chunk = height // size
        src, buf, out = gwb if stage == 0 else summed[stage - 1], gathered[stage], summed[stage]
        rs_s, rs_r, ag_s, ag_r = psems[4 * stage : 4 * stage + 4]

        def part(q):
            return pl.ds(pl.multiple_of(q * chunk, chunk), chunk)

        for step in range(1, size):
            _, other, peer = stage_peer(stage, step)
            remote(src.at[part(other), :], buf.at[step], rs_s.at[step], rs_r.at[step], {"blk": peer}).start()
        if stage == 0:
            for b in range(blocks + lag - tail, blocks):
                finish(b)
        digit, _, _ = stage_peer(stage, 1)
        if stage == 0:
            total = gw[part(digit), :]
        else:
            total = src[part(digit), :].astype(F32)
        for step in range(1, size):
            _, _, peer = stage_peer(stage, step)
            remote(buf.at[step], buf.at[step], rs_s.at[step], rs_r.at[step], {"blk": peer}).wait_recv()
            total = total + buf[step].astype(F32)
        out[part(digit), :] = total.astype(BF)
        for step in range(1, size):
            _, _, peer = stage_peer(stage, step)
            piece = out.at[part(digit), :]
            remote(piece, piece, ag_s.at[step], ag_r.at[step], {"blk": peer}).start()
        for step in range(1, size):
            _, other, peer = stage_peer(stage, size - step)
            piece = out.at[part(other), :]
            remote(piece, piece, ag_s.at[step], ag_r.at[step], {"blk": peer}).wait_recv()
    gw[...] = (summed[-1] if stages else gwb)[...].astype(F32)

    for stage in range(stages):
        size = factors[stage]
        chunk = height // size
        src, buf, out = gwb if stage == 0 else summed[stage - 1], gathered[stage], summed[stage]
        rs_s, rs_r, ag_s, ag_r = psems[4 * stage : 4 * stage + 4]
        for step in range(1, size):
            _, other, peer = stage_peer(stage, step)
            remote(buf.at[step], buf.at[step], rs_s.at[step], rs_r.at[step], {"blk": peer}).wait_send()
            remote(buf.at[step], buf.at[step], ag_s.at[step], ag_r.at[step], {"blk": peer}).wait_send()
    for step in range(1, nz):
        d = lax.rem(me + step, nz)
        remote(w.at[cols(d), :], wz.at[:, cols(me)], ws.at[step], wr.at[step], {"feat": d}).wait_send()

    def drain(b, carry):
        line_drain(xg, xs, xl, xr, b)
        line_drain(gg, zs, zl, zr, b)
        for k in far:
            remote(hid[k].at[b], hid[k].at[b], hs.at[k, b], hr.at[k, b], {"blk": blk_at(reach - k)}).wait_send()
            remote(sent.at[k, b], got.at[k, b], gs.at[k, b], gr.at[k, b], {"blk": blk_at(k - reach)}).wait_send()
        return carry

    lax.fori_loop(0, blocks, drain, 0)


def on_device(nb, nz, x, w, tv, tr, tc, cnt, go):
    offs, slots, side = tv.shape[1], tv.shape[2], tv.shape[-1]
    height, width = x.shape
    blocks = height // side
    depth, out_width = w.shape
    factors = stage_factors(nb, depth)
    dims = (nb, nz, offs, slots, blocks, side, width, 3, tuple(factors))
    vmem = pl.BlockSpec(memory_space=pltpu.VMEM)
    smem = pl.BlockSpec(memory_space=pltpu.SMEM)
    dma = pltpu.SemaphoreType.DMA
    psems = []
    for f in factors:
        psems += [dma((f,))] * 4
    line = [dma((nz, blocks))] * 3
    banded = [dma((offs, blocks))] * 2
    return pl.pallas_call(
        functools.partial(layer_kernel, dims),
        out_shape=(
            jax.ShapeDtypeStruct((height, out_width), BF),
            jax.ShapeDtypeStruct((height, width), BF),
            jax.ShapeDtypeStruct((depth, out_width), F32),
        ),
        in_specs=[vmem, vmem, vmem, smem, smem, smem, vmem],
        out_specs=(vmem, vmem, vmem),
        scratch_shapes=[
            pltpu.VMEM((height, nz * width), BF),
            pltpu.VMEM((width, nz * out_width), BF),
            pltpu.VMEM((offs, slots, side, side), BF),
            pltpu.VMEM((offs, slots, side, out_width), F32),
            pltpu.VMEM((blocks, side, out_width), BF),
            pltpu.VMEM((offs, blocks, side, out_width), BF),
            pltpu.VMEM((offs, blocks, side, out_width), BF),
            pltpu.VMEM((height, nz * out_width), BF),
            pltpu.VMEM((depth, out_width), BF),
        ]
        + [pltpu.VMEM((blocks, side, out_width), BF)] * offs
        + [pltpu.VMEM((f, depth // f, out_width), BF) for f in factors]
        + [pltpu.VMEM((depth, out_width), BF) for f in factors]
        + line
        + [dma((nz,)), dma((nz,))]
        + banded
        + banded
        + line
        + psems,
        compiler_params=pltpu.CompilerParams(
            collective_id=0, has_side_effects=True, vmem_limit_bytes=40 * 1024 * 1024
        ),
    )(x, w, tv, tr, tc, cnt, go)


def solution(mesh):
    return jax.shard_map(
        functools.partial(on_device, mesh.shape["blk"], mesh.shape["feat"]),
        mesh=mesh,
        in_specs=(
            P("blk", "feat"),
            P(None, "feat"),
            P("blk", None, None, None, None),
            P("blk", None, None),
            P("blk", None, None),
            P("blk", None),
            P("blk", "feat"),
        ),
        out_specs=(P("blk", "feat"), P("blk", "feat"), P(None, "feat")),
        check_vma=False,
    )
```

time: 217 us -> 86 us (0.40)
  waiting for transfers between devices: 136 us -> 0 us
  Pallas kernels: 0 us -> 76.8 us
  matrix products: 17.6 us -> 0 us
  other arithmetic: 14.8 us -> 0 us
  starting transfers between devices: 14.4 us -> 0 us
  between operations: 14.4 us -> 0.65 us
  local copies, waits for them, and re-layouts: 19.5 us -> 8.25 us
    pallas_call x0 -> x1, Pallas kernels: none -> 76.8 us  [on_device(): pl.pallas_call(functools.partial(layer_kernel, dims), out_shape=(jax.Shap...]
    psum x1 -> x0, waiting for transfers between devices: 52.1 us -> none  [on_device(): grad_w = lax.psum(weight_term, 'blk')]
    reduce_scatter x1 -> x0, waiting for transfers between devices: 43.6 us -> none  [on_device(): lax.psum_scatter(partial_grad, 'feat', scatter_dimension=1, tiled=True)]
    all_gather x1 -> x0, waiting for transfers between devices: 19.6 us -> none  [on_device(): full_feats = lax.all_gather(node_feats, 'feat', axis=1, tiled=True)]
    ppermute x12 -> x0, waiting for transfers between devices: 19.6 us -> none  [shifted(): return lax.ppermute(block, axis, route)]
    dot_general x23 -> x0, matrix products: 17.6 us -> none  [the longest x4 4.6 us: on_device(): jnp.einsum('cs,sif->cif', target_onehot, received, precision=lax.Precisio...]
    ppermute x12 -> x0, starting transfers between devices: 14.3 us -> none  [shifted(): return lax.ppermute(block, axis, route)]
    gather x10 -> x0, local copies, waits for them, and re-layouts: 6.84 us -> none  [the longest x5 3.73 us: slot_products(): picked = jnp.take(grad_blocks, tile_row[0, offset], axis=0)]
  transfers between devices with their start and end apart: 15 -> 0, of which waited for: 7 -> 0; matrix products, arithmetic and copies ran while one was open for 17% -> 0% of each run, Pallas kernels for 0% -> 0%
where the time goes in v1:
time: 86 us; the launch traced here: 85.7 us
  Pallas kernels  76.8 us (89%)
  local copies, waits for them, and re-layouts  8.25 us (10%)
    pallas_call x1, Pallas kernels, on_device(): pl.pallas_call(functools.partial(layer_kernel, dims), out_shape=(jax.Shap...  76.8 us
    unnamed x15, local copies, waits for them, and re-layouts  8.25 us

profile of v1, /device:TPU:0, one launch (start us, length us, event | category | flops | bytes accessed | tf_op | source)
XLA Modules:
  0.0 85.7 jit_solution(44737942821259242)
XLA Ops:
  0.6 0.7 copy.10.tr
  1.3 0.7 copy.11.tc
  2.0 0.0 copy-start
  2.0 1.3 %copy-done = bf16[1,5,8,128,128]{4,3,2,1,0:T(8,128)(2,1)S(1)} copy-done((bf16[1,5,8,128,128]{4,3,2,1,0:T(8,128)(2,1)S(1)}, bf16[1,5,8,128,128]{4,3,2,1,0:T(8,128)(2,1)}, u32[]{:S(2)}) %copy-start) | copy-done | bytes 1310744
  3.3 0.0 copy-start.1
  3.3 0.9 %copy-done.1 = bf16[1024,128]{1,0:T(8,128)(2,1)S(1)} copy-done((bf16[1024,128]{1,0:T(8,128)(2,1)S(1)}, bf16[1024,128]{1,0:T(8,128)(2,1)}, u32[]{:S(2)}) %copy-start.1) | copy-done | bytes 262168
  4.3 0.0 copy-start.2
  4.3 0.9 %copy-done.2 = bf16[1024,128]{1,0:T(8,128)(2,1)S(1)} copy-done((bf16[1024,128]{1,0:T(8,128)(2,1)S(1)}, bf16[1024,128]{1,0:T(8,128)(2,1)}, u32[]{:S(2)}) %copy-start.2) | copy-done | bytes 262168
  5.2 0.0 copy-start.3
  5.2 0.9 %copy-done.3 = bf16[512,128]{1,0:T(8,128)(2,1)S(1)} copy-done((bf16[512,128]{1,0:T(8,128)(2,1)S(1)}, bf16[512,128]{1,0:T(8,128)(2,1)}, u32[]{:S(2)}) %copy-start.3) | copy-done | bytes 131096
  6.1 0.0 copy-start.4
  6.1 0.7 copy-done.4
  6.8 76.8 %shard_map.94 = (bf16[1024,128]{1,0:T(8,128)(2,1)S(1)}, bf16[1024,128]{1,0:T(8,128)(2,1)S(1)}, f32[512,128]{1,0:T(8,128)S(1)}) custom-call(bf16[1024,128]{1,0:T(8,128)(2,1)S(1)} %copy-done.1, bf16[512,128]{1,0:T(8,128)(2,1)S(1)} %copy-done.3, bf16[1,5,8,128,128]{4,3,2,1,0:T(8,128)(2,1)S(1)} %copy-done, s32[1,5,8]{2,1,0:T(8,128)S(1)} %copy.10.tr, ...), custom_call_target="tpu_custom_call" | custom-call | tf_op jit(solution)/shard_map/pallas_call | solution.py:324
  83.6 0.7 copy.15
  84.3 0.7 copy.16
  85.0 0.7 copy.17
Async XLA Ops:
  2.0 1.3 %copy-start = (bf16[1,5,8,128,128]{4,3,2,1,0:T(8,128)(2,1)S(1)}, bf16[1,5,8,128,128]{4,3,2,1,0:T(8,128)(2,1)}, u32[]{:S(2)}) copy-start(bf16[1,5,8,128,128]{4,3,2,1,0:T(8,128)(2,1)} %tv.1) | copy-start | bytes 3932164
  3.3 0.9 %copy-start.1 = (bf16[1024,128]{1,0:T(8,128)(2,1)S(1)}, bf16[1024,128]{1,0:T(8,128)(2,1)}, u32[]{:S(2)}) copy-start(bf16[1024,128]{1,0:T(8,128)(2,1)} %x.1) | copy-start | bytes 786436
  4.3 0.9 %copy-start.2 = (bf16[1024,128]{1,0:T(8,128)(2,1)S(1)}, bf16[1024,128]{1,0:T(8,128)(2,1)}, u32[]{:S(2)}) copy-start(bf16[1024,128]{1,0:T(8,128)(2,1)} %go.1) | copy-start | bytes 786436
  5.2 0.9 %copy-start.3 = (bf16[512,128]{1,0:T(8,128)(2,1)S(1)}, bf16[512,128]{1,0:T(8,128)(2,1)}, u32[]{:S(2)}) copy-start(bf16[512,128]{1,0:T(8,128)(2,1)} %w.1) | copy-start | bytes 393220
  6.1 0.7 copy-start.4

commit v2 on v1

--- a/solution.py
+++ b/solution.py
@@ -28,29 +28,48 @@
 
 
 def layer_kernel(
-    dims, x, w, tv, tr, tc, cnt, go, y, gx, gw,
-    xg, wz, tt, prod, gp, sent, got, gg, gwb, *rest
+    dims, x, w_in, tv_in, tr, tc, cnt, go_in, y, gx, gw,
+    xg, wz, w, tv, go, tt, prod, gp, sent, got, gg, gwb, *rest
 ):
     nb, nz, offs, slots, blocks, side, width, ahead, factors = dims
     stages = len(factors)
     hid, rest = rest[:offs], rest[offs:]
     gathered, summed = rest[:stages], rest[stages : 2 * stages]
-    (xs, xr, xl, ws, wr, hs, hr, gs, gr, zs, zr, zl) = rest[2 * stages : 2 * stages + 12]
-    psems = rest[2 * stages + 12 :]
+    (xs, xr, xl, ws, wr, hs, hr, gs, gr, zs, zr, zl, near) = rest[2 * stages : 2 * stages + 13]
+    psems = rest[2 * stages + 13 :]
     reach = (offs - 1) // 2
-    far = [k for k in range(offs) if k != reach]
     per_block = slots // blocks
     me = lax.axis_index("feat")
     own = lax.axis_index("blk")
+    turn = 1 - 2 * lax.rem(own, 2)
+    OWN, PAIR, CROSS, AHEAD, BEHIND = range(5)
+    lean = (0, 1, -1, 2, -2)
+
+    def offset_of(role):
+        return reach + lean[role] * turn
+
+    def owner_at(role):
+        return {"blk": lax.rem(own + lean[role] * turn + nb, nb)}
+
+    local = [
+        pltpu.make_async_copy(w_in, w, near.at[0]),
+        pltpu.make_async_copy(x, xg.at[:, pl.ds(pl.multiple_of(me * width, width), width)], near.at[1]),
+        pltpu.make_async_copy(
+            w_in.at[pl.ds(pl.multiple_of(me * width, width), width), :],
+            wz.at[:, pl.ds(pl.multiple_of(me * w.shape[1], w.shape[1]), w.shape[1])],
+            near.at[2],
+        ),
+        pltpu.make_async_copy(tv_in.at[0], tv, near.at[3]),
+        pltpu.make_async_copy(go_in, go, near.at[4]),
+    ]
+    for copy in local:
+        copy.start()
 
     def rows(b):
         return pl.ds(pl.multiple_of(b * side, side), side)
 
     def cols(z):
         return pl.ds(pl.multiple_of(z * width, width), width)
-
-    def blk_at(distance):
-        return lax.rem(own + distance + nb, nb)
 
     def stage_peer(stage, step):
         stride = 1
@@ -66,8 +85,8 @@
     for step in range(1, nz):
         pl.semaphore_signal(barrier, inc=1, device_id={"feat": lax.rem(me + step, nz)}, device_id_type=MESH)
         greeted += 1
-    for k in far if stages > 1 else ():
-        pl.semaphore_signal(barrier, inc=1, device_id={"blk": blk_at(k - reach)}, device_id_type=MESH)
+    for role in (PAIR, AHEAD, BEHIND) if stages > 1 else ():
+        pl.semaphore_signal(barrier, inc=1, device_id=owner_at(role), device_id_type=MESH)
         greeted += 1
     for stage in range(stages):
         for step in range(1, factors[stage]):
@@ -130,49 +149,71 @@
         line_send(x_piece, xg, xs, xr, b)
     for step in range(1, nz):
         d = lax.rem(me + step, nz)
-        remote(w.at[cols(d), :], wz.at[:, cols(me)], ws.at[step], wr.at[nz - step], {"feat": d}).start()
-    xg[:, cols(me)] = x[...]
-    wz[:, cols(me)] = w[cols(me), :]
+        remote(w_in.at[cols(d), :], wz.at[:, cols(me)], ws.at[step], wr.at[nz - step], {"feat": d}).start()
+    for copy in local[:4]:
+        copy.wait()
+
+    landing = {PAIR: PAIR, AHEAD: BEHIND, BEHIND: AHEAD}
+
+    def hid_copy(role, b):
+        return remote(hid[OWN].at[b], hid[landing[role]].at[b], hs.at[role, b], hr.at[landing[role], b], owner_at(role))
+
+    def hid_wait(role, b):
+        remote(hid[role].at[b], hid[role].at[b], hs.at[role, b], hr.at[role, b], owner_at(PAIR)).wait_recv()
+
+    def hid_passed(b):
+        return remote(hid[AHEAD].at[b], hid[CROSS].at[b], hs.at[CROSS, b], hr.at[CROSS, b], owner_at(PAIR))
+
+    def hid_relay(b):
+        hid_wait(AHEAD, b)
+        hid_passed(b).start()
 
     def forward_step(b, carry):
         @pl.when(b + ahead < blocks)
         def _():
             line_send(x_piece, xg, xs, xr, b + ahead)
 
-        for k in range(offs):
+        for role in range(offs):
             for s in range(per_block):
                 slot = b * per_block + s
-                tt[k, slot] = tv[0, k, slot].T
+                tt[role, slot] = tv[offset_of(role), slot].T
         line_recv(xg, xl, xr, b)
-        hid[reach][b] = jnp.dot(xg[rows(b), :], w[...], preferred_element_type=F32).astype(BF)
-        for k in far:
-            remote(
-                hid[reach].at[b], hid[k].at[b], hs.at[k, b], hr.at[k, b], {"blk": blk_at(reach - k)}
-            ).start()
+        hid[OWN][b] = jnp.dot(xg[rows(b), :], w[...], preferred_element_type=F32).astype(BF)
+        hid_copy(PAIR, b).start()
+        hid_copy(AHEAD, b).start()
+        hid_copy(BEHIND, b).start()
+
+        @pl.when(b >= 1)
+        def _():
+            hid_relay(b - 1)
+
         return carry
 
     lax.fori_loop(0, blocks, forward_step, 0)
 
-    def forward_products(k):
+    hid_relay(blocks - 1)
+
+    def forward_products(role):
+        k = offset_of(role)
         for s in range(slots):
-            prod[k, s] = jnp.dot(tv[0, k, s], hid[k][tc[0, k, s]], preferred_element_type=F32)
-
-    forward_products(reach)
-    for k in far:
+            prod[role, s] = jnp.dot(tv[k, s], hid[role][tc[k, 0, s]], preferred_element_type=F32)
+
+    forward_products(OWN)
+    forward_products(AHEAD)
+    for role in (PAIR, BEHIND, CROSS):
         for b in range(blocks):
-            remote(
-                hid[k].at[b], hid[k].at[b], hs.at[k, b], hr.at[k, b], {"blk": blk_at(k - reach)}
-            ).wait_recv()
-        forward_products(k)
+            hid_wait(role, b)
+        forward_products(role)
+    local[4].wait()
 
     def weight_of(table, k, s, b):
-        return jnp.where((table[0, k, s] == b) & (s < cnt[0, k]), 1.0, 0.0).astype(F32)
+        return jnp.where((table[k, 0, s] == b) & (s < cnt[0, k]), 1.0, 0.0).astype(F32)
 
     def pointwise(b, carry):
-        v = hid[reach][b].astype(F32)
-        for k in range(offs):
+        v = hid[OWN][b].astype(F32)
+        for role in range(offs):
             for s in range(slots):
-                v = v + prod[k, s] * weight_of(tr, k, s, b)
+                v = v + prod[role, s] * weight_of(tr, offset_of(role), s, b)
         sigma = jax.nn.sigmoid(v)
         y[rows(b), :] = (v * sigma).astype(BF)
         slope = sigma * (1.0 + v * (1.0 - sigma))
@@ -181,29 +222,47 @@
 
     lax.fori_loop(0, blocks, pointwise, 0)
 
-    for k in range(offs):
+    for role in range(offs):
         for s in range(slots):
-            prod[k, s] = jnp.dot(tt[k, s], gp[tr[0, k, s]], preferred_element_type=F32)
-
-    def column_sum(k, c, start):
+            prod[role, s] = jnp.dot(tt[role, s], gp[tr[offset_of(role), 0, s]], preferred_element_type=F32)
+
+    def column_sum(role, c, start):
         total = start
         for s in range(slots):
-            term = prod[k, s] * weight_of(tc, k, s, c)
+            term = prod[role, s] * weight_of(tc, offset_of(role), s, c)
             total = term if total is None else total + term
         return total
 
+    target = {PAIR: PAIR, CROSS: PAIR, AHEAD: AHEAD, BEHIND: BEHIND}
+    arrives = {PAIR: PAIR, CROSS: CROSS, AHEAD: BEHIND, BEHIND: AHEAD}
+
+    def sum_copy(role, c):
+        return remote(
+            sent.at[role, c], got.at[arrives[role], c], gs.at[role, c], gr.at[arrives[role], c], owner_at(target[role])
+        )
+
+    def sum_wait(role, c):
+        remote(got.at[role, c], got.at[role, c], gs.at[role, c], gr.at[role, c], owner_at(PAIR)).wait_recv()
+
+    def send_sum(role, c):
+        sent[role, c] = column_sum(role, c, None).astype(BF)
+        sum_copy(role, c).start()
+
+    def send_joint(c):
+        sum_wait(CROSS, c)
+        sent[AHEAD, c] = column_sum(AHEAD, c, got[CROSS, c].astype(F32)).astype(BF)
+        sum_copy(AHEAD, c).start()
+
     gw[...] = jnp.zeros_like(gw)
 
     def gg_piece(b):
         return gg.at[rows(b), cols(me)]
 
     def make_grad(b):
-        total = column_sum(reach, b, gp[b].astype(F32))
-        for k in far:
-            remote(
-                sent.at[k, b], got.at[k, b], gs.at[k, b], gr.at[k, b], {"blk": blk_at(reach - k)}
-            ).wait_recv()
-            total = total + got[k, b].astype(F32)
+        total = column_sum(OWN, b, gp[b].astype(F32))
+        for role in (PAIR, BEHIND, AHEAD):
+            sum_wait(role, b)
+            total = total + got[role, b].astype(F32)
         grad = total.astype(BF)
         gg[rows(b), cols(me)] = grad
         line_send(gg_piece, gg, zs, zr, b)
@@ -220,18 +279,20 @@
     for step in range(1, nz):
         d = lax.rem(me + step, nz)
         piece = wz.at[:, cols(d)]
-        remote(w.at[cols(d), :], piece, ws.at[step], wr.at[step], {"feat": d}).wait_recv()
-
-    lag, tail = 1, 3
+        remote(w_in.at[cols(d), :], piece, ws.at[step], wr.at[step], {"feat": d}).wait_recv()
+
+    lag, tail = 2, 4
 
     def backward_step(c, carry):
         @pl.when(c < blocks)
         def _():
-            for k in far:
-                sent[k, c] = column_sum(k, c, None).astype(BF)
-                remote(
-                    sent.at[k, c], got.at[k, c], gs.at[k, c], gr.at[k, c], {"blk": blk_at(k - reach)}
-                ).start()
+            send_sum(CROSS, c)
+            send_sum(BEHIND, c)
+            send_sum(PAIR, c)
+
+        @pl.when((c >= 1) & (c <= blocks))
+        def _():
+            send_joint(c - 1)
 
         @pl.when(c >= lag)
         def _():
@@ -293,14 +354,16 @@
             remote(buf.at[step], buf.at[step], ag_s.at[step], ag_r.at[step], {"blk": peer}).wait_send()
     for step in range(1, nz):
         d = lax.rem(me + step, nz)
-        remote(w.at[cols(d), :], wz.at[:, cols(me)], ws.at[step], wr.at[step], {"feat": d}).wait_send()
+        remote(w_in.at[cols(d), :], wz.at[:, cols(me)], ws.at[step], wr.at[step], {"feat": d}).wait_send()
 
     def drain(b, carry):
         line_drain(xg, xs, xl, xr, b)
         line_drain(gg, zs, zl, zr, b)
-        for k in far:
-            remote(hid[k].at[b], hid[k].at[b], hs.at[k, b], hr.at[k, b], {"blk": blk_at(reach - k)}).wait_send()
-            remote(sent.at[k, b], got.at[k, b], gs.at[k, b], gr.at[k, b], {"blk": blk_at(k - reach)}).wait_send()
+        for role in (PAIR, AHEAD, BEHIND):
+            hid_copy(role, b).wait_send()
+        hid_passed(b).wait_send()
+        for role in (PAIR, CROSS, AHEAD, BEHIND):
+            sum_copy(role, b).wait_send()
         return carry
 
     lax.fori_loop(0, blocks, drain, 0)
@@ -314,6 +377,7 @@
     factors = stage_factors(nb, depth)
     dims = (nb, nz, offs, slots, blocks, side, width, 3, tuple(factors))
     vmem = pl.BlockSpec(memory_space=pltpu.VMEM)
+    hbm = pl.BlockSpec(memory_space=pltpu.HBM)
     smem = pl.BlockSpec(memory_space=pltpu.SMEM)
     dma = pltpu.SemaphoreType.DMA
     psems = []
@@ -328,11 +392,14 @@
             jax.ShapeDtypeStruct((height, width), BF),
             jax.ShapeDtypeStruct((depth, out_width), F32),
         ),
-        in_specs=[vmem, vmem, vmem, smem, smem, smem, vmem],
+        in_specs=[hbm, hbm, hbm, smem, smem, smem, hbm],
         out_specs=(vmem, vmem, vmem),
         scratch_shapes=[
             pltpu.VMEM((height, nz * width), BF),
             pltpu.VMEM((width, nz * out_width), BF),
+            pltpu.VMEM((depth, out_width), BF),
+            pltpu.VMEM((offs, slots, side, side), BF),
+            pltpu.VMEM((height, out_width), BF),
             pltpu.VMEM((offs, slots, side, side), BF),
             pltpu.VMEM((offs, slots, side, out_width), F32),
             pltpu.VMEM((blocks, side, out_width), BF),
@@ -349,11 +416,12 @@
         + banded
         + banded
         + line
+        + [dma((5,))]
         + psems,
         compiler_params=pltpu.CompilerParams(
-            collective_id=0, has_side_effects=True, vmem_limit_bytes=40 * 1024 * 1024
+            collective_id=0, has_side_effects=True, vmem_limit_bytes=63 * 1024 * 1024
         ),
-    )(x, w, tv, tr, tc, cnt, go)
+    )(x, w, tv, jnp.swapaxes(tr, 0, 1), jnp.swapaxes(tc, 0, 1), cnt, go)
 
 
 def solution(mesh):

time: 86 us -> 84 us (0.977)
  local copies, waits for them, and re-layouts: 8.25 us -> 5.01 us
  Pallas kernels: 76.8 us -> 78.1 us
    unnamed x15 -> x3, local copies, waits for them, and re-layouts: 8.25 us -> 5.01 us
    pallas_call x1, Pallas kernels: 76.8 us -> 78.1 us  [on_device(): pl.pallas_call(functools.partial(layer_kernel, dims), out_shape=(jax.Shap...]
where the time goes in v2:
time: 84 us; the launch traced here: 83.8 us
  Pallas kernels  78.1 us (93%)
  local copies, waits for them, and re-layouts  5.01 us (6%)
    pallas_call x1, Pallas kernels, on_device(): pl.pallas_call(functools.partial(layer_kernel, dims), out_shape=(jax.Shap...  78.1 us
    unnamed x3, local copies, waits for them, and re-layouts  5.01 us

profile of v2, /device:TPU:0, one launch (start us, length us, event | category | flops | bytes accessed | tf_op | source)
XLA Modules:
  0.0 83.8 jit_solution(17719091344102027336)
XLA Ops:
  0.6 78.1 %shard_map.94 = (bf16[1024,128]{1,0:T(8,128)(2,1)}, bf16[1024,128]{1,0:T(8,128)(2,1)}, f32[512,128]{1,0:T(8,128)}) custom-call(bf16[1024,128]{1,0:T(8,128)(2,1)} %x.1, bf16[512,128]{1,0:T(8,128)(2,1)} %w_in.1, bf16[1,5,8,128,128]{4,3,2,1,0:T(8,128)(2,1)} %tv_in.1, s32[5,1,8]{2,1,0:T(1,128)} %bitcast.2, s32[5,1,8]{2,1,0:T(1,128)} %bitcast.3, s32[1,5]{1,0:T(1,128)} %cnt.1, ...), custom_call_target="tpu_custom_call" | custom-call | tf_op jit(solution)/shard_map/pallas_call | solution.py:388
  78.7 1.7 %copy.13 = bf16[1024,128]{1,0:T(8,128)(2,1)} copy(bf16[1024,128]{1,0:T(8,128)(2,1)} %get-tuple-element.6) | data formatting | bytes 524288
  80.4 1.7 %copy.14 = bf16[1024,128]{1,0:T(8,128)(2,1)} copy(bf16[1024,128]{1,0:T(8,128)(2,1)} %get-tuple-element.7) | data formatting | bytes 524288
  82.1 1.7 %copy.15 = f32[512,128]{1,0:T(8,128)} copy(f32[512,128]{1,0:T(8,128)} %get-tuple-element.8) | data formatting | bytes 524288
